TPU v7x, 32 devices: a whole 2x2x4 slice. The times are simulated.
32 devices in a mesh: dp: 16 (over z, x, core), tensor: 2 (over y).
Axes of the slice: x: 2, y: 2, z: 4, core: 2. Of those that a mesh axis runs over, the one named last changes fastest.
Arguments:
- tokens: bfloat16 [32768, 512], P('dp'), may hold values from -6 to 6
- seq_lengths: int32 [32], P('dp'), may hold values from 1024 to 1024, as said below
- packed_slot: int32 [32768], P('dp'), may hold values from 0 to 32767, as said below
- out_grad: bfloat16 [32768, 512], P('dp'), may hold values from -6 to 6
- qkv_weight: bfloat16 [3, 512, 512], P(None, None, 'tensor'), may hold values from -0.25 to 0.25
- out_weight: bfloat16 [512, 512], P('tensor'), may hold values from -2 to 2
- up_weight: bfloat16 [512, 2048], P(None, 'tensor'), may hold values from -0.25 to 0.25
- down_weight: bfloat16 [2048, 512], P('tensor'), may hold values from -0.125 to 0.125
- gain_first: float32 [512], replicated, may hold values from 0.1 to 1.9
- shift_first: float32 [512], replicated, may hold values from -0.6 to 0.6
- gain_second: float32 [512], replicated, may hold values from 0.1 to 1.9
- shift_second: float32 [512], replicated, may hold values from -0.6 to 0.6
- up_bias: float32 [2048], P('tensor'), may hold values from -12 to 12
Outputs:
- layer_out: bfloat16 [32768, 512], P('dp')
- grad_input: bfloat16 [32768, 512], P('dp')
- grad_qkv: float32 [3, 512, 512], P(None, None, 'tensor')
- grad_outproj: float32 [512, 512], P('tensor')
- grad_up: float32 [512, 2048], P(None, 'tensor')
- grad_down: float32 [2048, 512], P('tensor')
- grad_gain_first: float32 [512], replicated
- grad_shift_first: float32 [512], replicated
- grad_gain_second: float32 [512], replicated
- grad_shift_second: float32 [512], replicated
- grad_up_bias: float32 [2048], P('tensor')
Inputs may be any that keep to these rules, and one draw needn't show every extreme that they name: Each pair seq_lengths[2b], seq_lengths[2b+1] sums to 2048; every length is a multiple of 64; some pair is (1024, 1024). packed_slot is a permutation of the rows; of the 2048 rows of one index of dp, exactly 128 have packed_slot // 2048 equal to each index of dp.
All inputs are finite; a program needn't handle non-finite values.
Results may differ from a plain program's by a relative error of at most 0.015.
Values may be sent and summed in bfloat16 or wider, within the bound.
No kernel may reach another device: no remote copies, remote signals or barrier semaphores. Data moves between devices by JAX's collectives and lax.ppermute only.
A program may use at most 192 MiB of HBM per device.

v0:
```python
import jax
import jax.numpy as jnp
from jax import lax
from jax.sharding import PartitionSpec as P

HD = 64
BLK = 64


def layer_norm(value, gain, shift):
    mean = jnp.mean(value, axis=-1, keepdims=True)
    cent = value - mean
    var = jnp.mean(cent * cent, axis=-1, keepdims=True)
    return cent * lax.rsqrt(var + 1e-05) * gain + shift


def feature(value):
    return jnp.where(value > 0, value + 1.0, jnp.exp(jnp.minimum(value, 0.0)))


def feature_slope(value):
    return jnp.where(value > 0, 1.0, jnp.exp(jnp.minimum(value, 0.0)))


def silu_slope(value):
    sigma = jax.nn.sigmoid(value)
    return sigma * (1.0 + value * (1.0 - sigma))


def rounded(value):
    return lax.optimization_barrier(value.astype(jnp.bfloat16)).astype(jnp.float32)


def linear_attention(q_feat, k_feat, v_feat, stretch_seq):
    best = lax.Precision.HIGHEST
    nblk = q_feat.shape[0] // BLK
    query = q_feat.reshape(nblk, BLK, -1, HD)
    keys = k_feat.reshape(nblk, BLK, -1, HD)
    values = v_feat.reshape(nblk, BLK, -1, HD)
    outer = jnp.einsum("cjhe,cjhf->chef", keys, values, precision=best)
    ksum = jnp.sum(keys, axis=1)
    index = jnp.arange(nblk)
    mixing = (
        (index[None, :] < index[:, None]) & (stretch_seq[None, :] == stretch_seq[:, None])
    ).astype(jnp.float32)
    state = jnp.einsum("cd,dhef->chef", mixing, outer, precision=best)
    zsum = jnp.einsum("cd,dhe->che", mixing, ksum, precision=best)
    scores = jnp.einsum("cihe,cjhe->chij", query, keys, precision=best)
    lower = (jnp.arange(BLK)[None, :] <= jnp.arange(BLK)[:, None]).astype(jnp.float32)
    scores = scores * lower
    numer = jnp.einsum("cihe,chef->cihf", query, state, precision=best)
    numer = numer + jnp.einsum("chij,cjhf->cihf", scores, values, precision=best)
    denom = jnp.einsum("cihe,che->cih", query, zsum, precision=best)
    denom = denom + jnp.transpose(jnp.sum(scores, axis=-1), (0, 2, 1)) + 1e-06
    result = numer / denom[..., None]
    return result.reshape(nblk * BLK, -1)


def per_device(
    tokens,
    seq_lengths,
    packed_slot,
    out_grad,
    qkv_weight,
    out_weight,
    up_weight,
    down_weight,
    gain_first,
    shift_first,
    gain_second,
    shift_second,
    up_bias,
):
    rows = tokens.shape[0]
    count = lax.axis_size("dp")
    slot = rows // count
    order = jnp.argsort(packed_slot)
    sent = (
        tokens[order].reshape(count, slot, -1),
        out_grad[order].reshape(count, slot, -1),
        packed_slot[order].reshape(count, slot),
    )
    got_rows, got_grads, got_slots = (
        lax.all_to_all(sent[0], "dp", split_axis=0, concat_axis=0, tiled=True),
        lax.all_to_all(sent[1], "dp", split_axis=0, concat_axis=0, tiled=True),
        lax.all_to_all(sent[2], "dp", split_axis=0, concat_axis=0, tiled=True),
    )
    local_pos = got_slots.reshape(rows) % rows
    arrange = jnp.argsort(local_pos)
    inputs = got_rows.reshape(rows, -1)[arrange].astype(jnp.float32)
    grad_low = got_grads.reshape(rows, -1)[arrange]
    nblk = rows // BLK
    stretch_seq = (jnp.arange(nblk) * BLK >= seq_lengths[0]).astype(jnp.int32)
    first, first_pull = jax.vjp(layer_norm, inputs, gain_first, shift_first)
    first_low = first.astype(jnp.bfloat16)
    projected = jnp.einsum("td,jdc->jtc", first_low, qkv_weight, preferred_element_type=jnp.float32)
    q_feat = rounded(feature(projected[0]))
    k_feat = rounded(feature(projected[1]))
    v_feat = rounded(projected[2])
    attended, attn_pull = jax.vjp(
        lambda a, b, c: linear_attention(a, b, c, stretch_seq), q_feat, k_feat, v_feat
    )
    attended_low = attended.astype(jnp.bfloat16)
    attn_part = jnp.dot(attended_low, out_weight, preferred_element_type=jnp.float32)
    middle = inputs + lax.psum(attn_part.astype(jnp.bfloat16), "tensor").astype(jnp.float32)
    second, second_pull = jax.vjp(layer_norm, middle, gain_second, shift_second)
    second_low = second.astype(jnp.bfloat16)
    hidden = jnp.dot(second_low, up_weight, preferred_element_type=jnp.float32) + up_bias
    active_low = jax.nn.silu(hidden).astype(jnp.bfloat16)
    ffn_part = jnp.dot(active_low, down_weight, preferred_element_type=jnp.float32)
    result = (
        middle + lax.psum(ffn_part.astype(jnp.bfloat16), "tensor").astype(jnp.float32)
    ).astype(jnp.bfloat16)
    grad_down = jnp.einsum("tf,td->fd", active_low, grad_low, preferred_element_type=jnp.float32)
    grad_active = jnp.einsum("td,fd->tf", grad_low, down_weight, preferred_element_type=jnp.float32)
    grad_hidden = (grad_active * silu_slope(hidden)).astype(jnp.bfloat16)
    grad_up = jnp.einsum("td,tf->df", second_low, grad_hidden, preferred_element_type=jnp.float32)
    grad_up_bias = jnp.sum(grad_hidden.astype(jnp.float32), axis=0)
    second_part = jnp.einsum(
        "tf,df->td", grad_hidden, up_weight, preferred_element_type=jnp.float32
    )
    grad_second = lax.psum(second_part.astype(jnp.bfloat16), "tensor").astype(jnp.float32)
    middle_norm, grad_gain_second, grad_shift_second = second_pull(grad_second)
    grad_middle = grad_low.astype(jnp.float32) + middle_norm
    middle_low = grad_middle.astype(jnp.bfloat16)
    grad_outproj = jnp.einsum(
        "tc,td->cd", attended_low, middle_low, preferred_element_type=jnp.float32
    )
    grad_attended = jnp.einsum(
        "td,cd->tc", middle_low, out_weight, preferred_element_type=jnp.float32
    )
    grad_qf, grad_kf, grad_vf = attn_pull(grad_attended)
    grad_proj = jnp.stack(
        [grad_qf * feature_slope(projected[0]), grad_kf * feature_slope(projected[1]), grad_vf]
    ).astype(jnp.bfloat16)
    grad_qkv = jnp.einsum("td,jtc->jdc", first_low, grad_proj, preferred_element_type=jnp.float32)
    first_part = jnp.einsum(
        "jtc,jdc->td", grad_proj, qkv_weight, preferred_element_type=jnp.float32
    )
    grad_first = lax.psum(first_part.astype(jnp.bfloat16), "tensor").astype(jnp.float32)
    input_norm, grad_gain_first, grad_shift_first = first_pull(grad_first)
    grad_inputs = (grad_middle + input_norm).astype(jnp.bfloat16)
    (
        grad_qkv,
        grad_outproj,
        grad_up,
        grad_down,
        grad_up_bias,
        grad_gain_first,
        grad_shift_first,
        grad_gain_second,
        grad_shift_second,
    ) = lax.psum(
        (
            grad_qkv,
            grad_outproj,
            grad_up,
            grad_down,
            grad_up_bias,
            grad_gain_first,
            grad_shift_first,
            grad_gain_second,
            grad_shift_second,
        ),
        "dp",
    )
    back = (
        result[local_pos].reshape(count, slot, -1),
        grad_inputs[local_pos].reshape(count, slot, -1),
    )
    got_out, got_input = (
        lax.all_to_all(back[0], "dp", split_axis=0, concat_axis=0, tiled=True),
        lax.all_to_all(back[1], "dp", split_axis=0, concat_axis=0, tiled=True),
    )
    undo = jnp.argsort(order)
    layer_out = got_out.reshape(rows, -1)[undo]
    grad_input = got_input.reshape(rows, -1)[undo]
    return (
        layer_out,
        grad_input,
        grad_qkv,
        grad_outproj,
        grad_up,
        grad_down,
        grad_gain_first,
        grad_shift_first,
        grad_gain_second,
        grad_shift_second,
        grad_up_bias,
    )


def solution(mesh):
    placed = (
        P("dp", None),
        P("dp"),
        P("dp"),
        P("dp", None),
        P(None, None, "tensor"),
        P("tensor", None),
        P(None, "tensor"),
        P("tensor", None),
        P(),
        P(),
        P(),
        P(),
        P("tensor"),
    )
    return jax.shard_map(
        per_device,
        mesh=mesh,
        in_specs=placed,
        out_specs=(
            P("dp", None),
            P("dp", None),
            P(None, None, "tensor"),
            P("tensor", None),
            P(None, "tensor"),
            P("tensor", None),
            P(),
            P(),
            P(),
            P(),
            P("tensor"),
        ),
        check_vma=False,
    )
```

profile of v0, /device:TPU:0, one launch (start us, length us, event | category | flops | bytes accessed | tf_op | source)
XLA Modules:
  0.0 935.9 jit_solution(12726560406458529215)
XLA Ops:
  13.1 20.6 %gather_fusion.1 = s32[2048]{0:T(1024)} fusion(s32[2048]{0:T(1024)S(1)} %copy-done.2, s32[2048]{0:T(1024)S(1)} %fusion.86), kind=kCustom, calls=%fused_computation.1 | custom fusion | bytes 24576 | tf_op jit(solution)/shard_map/gather | solution.py:81
  33.7 7.4 all-to-all-start.1
  41.0 9.2 gather_fusion
  56.3 11.1 %gather_fusion.5 = bf16[2048,512]{1,0:T(8,128)(2,1)} fusion(bf16[2048,512]{1,0:T(8,128)(2,1)} %param.16, s32[2048]{0:T(1024)S(1)} %fusion.86), kind=kCustom, calls=%fused_computation.5 | custom fusion | bytes 4202496 | tf_op jit(solution)/shard_map/gather | solution.py:80
  72.5 24.8 %all-to-all-done = bf16[16,128,512]{2,1,0:T(8,128)(2,1)S(1)} async-done(((bf16[16,128,512]{2,1,0:T(8,128)(2,1)}), bf16[16,128,512]{2,1,0:T(8,128)(2,1)S(1)}, u32[]{:S(2)}, u32[]{:S(2)}) %all-to-all-start) | async-done | bytes 2097184 | tf_op jit(solution)/shard_map/all_to_all | solution.py:84
  97.4 11.3 %all-to-all-start.3 = ((bf16[16,128,512]{2,1,0:T(8,128)(2,1)}), bf16[16,128,512]{2,1,0:T(8,128)(2,1)}, u32[]{:S(2)}, u32[]{:S(2)}) async-start(bf16[16,128,512]{2,1,0:T(8,128)(2,1)} %bitcast.114), calls=%async_computation.3 | async-start | bytes 4194304 | tf_op jit(solution)/shard_map/all_to_all | solution.py:85
  108.9 9.5 %gather_fusion.2 = bf16[2048,512]{1,0:T(8,128)(2,1)S(1)} fusion(bf16[2048,512]{1,0:T(8,128)(2,1)} %bitcast.113, s32[2048]{0:T(1024)S(1)} %fusion.87), kind=kCustom, calls=%fused_computation.2 | custom fusion | bytes 4202496 | tf_op jit(solution)/shard_map/gather | solution.py:90
  158.4 7.2 fusion.29
  178.8 11.3 %gather_fusion.6 = bf16[2048,512]{1,0:T(8,128)(2,1)} fusion(bf16[2048,512]{1,0:T(8,128)(2,1)} %bitcast.22, s32[2048]{0:T(1024)S(1)} %fusion.87), kind=kCustom, calls=%fused_computation.6 | custom fusion | bytes 4202496 | tf_op jit(solution)/shard_map/gather | solution.py:91
  190.1 53.0 %all-reduce.8.cloned.1.call-done = bf16[2048,512]{1,0:T(8,128)(2,1)} async-done(((bf16[2048,512]{1,0:T(8,128)(2,1)}), bf16[2048,512]{1,0:T(8,128)(2,1)}) %all-reduce.8.cloned.1.call-update) | async-done | bytes 2097168 | tf_op jit(solution)/shard_map/psum | solution.py:105
  269.5 56.8 %all-reduce.10.cloned.1.call-done = bf16[2048,512]{1,0:T(8,128)(2,1)} async-done(((bf16[2048,512]{1,0:T(8,128)(2,1)}), bf16[2048,512]{1,0:T(8,128)(2,1)}) %all-reduce.10.cloned.1.call-update) | async-done | bytes 2097168 | tf_op jit(solution)/shard_map/psum | solution.py:122
  343.6 15.5 %fusion.15 = f32[32,4,64,64]{3,2,1,0:T(8,128)} fusion(f32[32,4,64,64]{2,3,1,0:T(8,128)} %copy-done.30, f32[64,64]{0,1:T(8,128)S(1)} %fusion.79, f32[32,64,4,64]{1,0,3,2:T(8,128)} %reshape.276, f32[32,64,4]{1,2,0:T(4,128)S(1)} %copy-done.53), kind=kOutput, calls=%fused_computation.41 | convolution fusion | flops 403701760 | bytes 6340608 | tf_op jit(solution)/shard_map/transpose(jvp(chij,cjhf->cihf))/dot_general | solution.py:52
  359.1 13.6 %fusion.21 = f32[32,4,64,64]{2,3,1,0:T(8,128)} fusion(f32[32,4,64,64]{3,0,2,1:T(8,128)S(1)} %copy-done.22, f32[32,64,4,64]{1,0,3,2:T(8,128)S(1)} %copy-done.23, f32[32,64,4]{1,2,0:T(4,128)S(1)} %copy-done.53), kind=kOutput, calls=%fused_computation.47 | convolution fusion | flops 403177472 | bytes 6324224 | tf_op jit(solution)/shard_map/transpose(jvp(cihe,chef->cihf))/dot_general | solution.py:51
  379.5 7.5 fusion.19
  437.9 9.9 %add_bitcast_fusion = f32[32,64,4,64]{1,3,2,0:T(8,128)} fusion(f32[32,4,64,64]{2,3,1,0:T(8,128)} %fusion.21, f32[32,4,64,64]{2,3,1,0:T(8,128)} %fusion.19, f32[32,4,64]{2,1,0:T(4,128)S(1)} %copy.105, f32[32,4,64]{2,1,0:T(4,128)S(1)} %get-tuple-element.83, f32[64,64]{0,1:T(8,128)S(1)} %fusion.79, bf16[32,64,4,64]{3,2,1,0:T(4,128)(2,1)} %reshape.267), kind=kOutput, calls=%fused_computation.59 | convolution fusion | flops 405274624 | bytes 7421952 | tf_op jit(solution)/shard_map/transpose(jvp(cihe,cjhe->chij))/dot_general | solution.py:48
  468.5 107.7 %all-reduce.14.cloned.1.call-done = (bf16[2048,512]{1,0:T(8,128)(2,1)}, bf16[2048,512]{1,0:T(8,128)(2,1)}) async-done(((bf16[2048,512]{1,0:T(8,128)(2,1)}, bf16[2048,512]{1,0:T(8,128)(2,1)}), (bf16[2048,512]{1,0:T(8,128)(2,1)}, bf16[2048,512]{1,0:T(8,128)(2,1)})) %all-reduce.14.cloned.1.call-update) | async-done | bytes 4194320 | tf_op jit(solution)/shard_map/psum | solution.py:112
  589.1 11.1 %gather_fusion.7 = bf16[2048,512]{1,0:T(8,128)(2,1)} fusion(bf16[2048,512]{1,0:T(8,128)(2,1)} %get-tuple-element.80, s32[2048]{0:T(1024)S(1)} %broadcast_clamp_fusion), kind=kCustom, calls=%fused_computation.7 | custom fusion | bytes 4202496 | tf_op jit(solution)/shard_map/gather | solution.py:169
  616.9 11.1 %gather_fusion.3 = bf16[2048,512]{1,0:T(8,128)(2,1)} fusion(bf16[2048,512]{1,0:T(8,128)(2,1)} %get-tuple-element.81, s32[2048]{0:T(1024)S(1)} %broadcast_clamp_fusion), kind=kCustom, calls=%fused_computation.3 | custom fusion | bytes 4202496 | tf_op jit(solution)/shard_map/gather | solution.py:168
  628.0 19.3 %all-to-all-done.4 = bf16[16,128,512]{2,1,0:T(8,128)(2,1)} async-done(((bf16[16,128,512]{2,1,0:T(8,128)(2,1)}), bf16[16,128,512]{2,1,0:T(8,128)(2,1)}, u32[]{:S(2)}, u32[]{:S(2)}) %all-to-all-start.4) | async-done | bytes 2097184 | tf_op jit(solution)/shard_map/all_to_all | solution.py:173
  647.3 11.3 %all-to-all-start.2 = ((bf16[16,128,512]{2,1,0:T(8,128)(2,1)}), bf16[16,128,512]{2,1,0:T(8,128)(2,1)}, u32[]{:S(2)}, u32[]{:S(2)}) async-start(bf16[16,128,512]{2,1,0:T(8,128)(2,1)} %bitcast.115), calls=%async_computation.2 | async-start | bytes 4194304 | tf_op jit(solution)/shard_map/all_to_all | solution.py:172
  672.6 164.9 %all-reduce.12.cloned.1.call-done = (f32[3,512,256]{1,2,0:T(8,128)}, f32[256,512]{1,0:T(8,128)}, f32[512,1024]{1,0:T(8,128)}, f32[1024,512]{1,0:T(8,128)}) async-done(((f32[3,512,256]{1,2,0:T(8,128)}, f32[256,512]{1,0:T(8,128)}, f32[512,1024]{1,0:T(8,128)}, f32[1024,512]{1,0:T(8,128)}), (f32[3,512,256]{1,2,0:T(8,128)}, f32[256,512]{1,0:T(8,128)}, f32[512,1024]{1,0:T(8,128)}, ...) | async-done | bytes 6291472 | tf_op jit(solution)/shard_map/psum | solution.py:153
  840.6 60.4 %all-reduce = (f32[512]{0:T(512)}, f32[512]{0:T(512)}, f32[512]{0:T(512)}, f32[512]{0:T(512)}, f32[1024]{0:T(1024)}) all-reduce(f32[512]{0:T(512)S(1)} %get-tuple-element.52, f32[512]{0:T(512)S(1)} %get-tuple-element.55, f32[512]{0:T(512)S(1)} %get-tuple-element.50, ...), channel_id=1, replica_groups=mesh['dp'=16,'tensor'=2] {'dp'}, use_global_device_ids=true, to_apply=%region_23.24 | all-reduce | flops 3072 | bytes 24576 | tf_op jit(solution)/shard_map/psum | solution.py:153
  901.0 11.1 %gather_fusion.8 = bf16[2048,512]{1,0:T(8,128)(2,1)} fusion(bf16[2048,512]{1,0:T(8,128)(2,1)} %bitcast.37, s32[2048]{0:T(1024)S(1)} %fusion.88), kind=kCustom, calls=%fused_computation.8 | custom fusion | bytes 4202496 | tf_op jit(solution)/shard_map/gather | solution.py:177
  912.1 11.2 %gather_fusion.4 = bf16[2048,512]{1,0:T(8,128)(2,1)} fusion(bf16[2048,512]{1,0:T(8,128)(2,1)} %bitcast.20, s32[2048]{0:T(1024)S(1)} %fusion.88), kind=kCustom, calls=%fused_computation.4 | custom fusion | bytes 4202496 | tf_op jit(solution)/shard_map/gather | solution.py:176
  (237 shorter events, 244.2 us)
Async XLA Ops:
  7.2 33.9 %copy-start = (bf16[2048,512]{1,0:T(8,128)(2,1)S(1)}, bf16[2048,512]{1,0:T(8,128)(2,1)}, u32[]{:S(2)}) copy-start(bf16[2048,512]{1,0:T(8,128)(2,1)} %param.13) | copy-start | bytes 6291460
  13.1 20.6 %copy-start.54 = (s32[2048]{0:T(1024)}, s32[2048]{0:T(1024)S(1)}, u32[]{:S(2)}) copy-start(s32[2048]{0:T(1024)S(1)} %get-tuple-element.14) | copy-start | bytes 24580
  33.7 16.6 %all-to-all-start.1 = ((s32[16,1,128]{2,1,0:T(1,128)}), s32[16,1,128]{2,1,0:T(1,128)S(1)}, u32[]{:S(2)}, u32[]{:S(2)}) async-start(s32[16,1,128]{2,1,0:T(1,128)} %bitcast.2), calls=%async_computation.1 | async-start | bytes 16384 | tf_op jit(solution)/shard_map/all_to_all | solution.py:86
  50.2 17.2 %copy-start.50 = (s32[16,1,128]{2,1,0:T(1,128)}, s32[16,1,128]{2,1,0:T(1,128)S(1)}, u32[]{:S(2)}) copy-start(s32[16,1,128]{2,1,0:T(1,128)S(1)} %all-to-all-done.1) | copy-start | bytes 24580
  50.2 47.1 %all-to-all-start = ((bf16[16,128,512]{2,1,0:T(8,128)(2,1)}), bf16[16,128,512]{2,1,0:T(8,128)(2,1)S(1)}, u32[]{:S(2)}, u32[]{:S(2)}) async-start(bf16[16,128,512]{2,1,0:T(8,128)(2,1)} %bitcast.116), calls=%async_computation | async-start | bytes 4194304 | tf_op jit(solution)/shard_map/all_to_all | solution.py:84
  97.4 81.4 %all-to-all-start.3 = ((bf16[16,128,512]{2,1,0:T(8,128)(2,1)}), bf16[16,128,512]{2,1,0:T(8,128)(2,1)}, u32[]{:S(2)}, u32[]{:S(2)}) async-start(bf16[16,128,512]{2,1,0:T(8,128)(2,1)} %bitcast.114), calls=%async_computation.3 | async-start | bytes 4194304 | tf_op jit(solution)/shard_map/all_to_all | solution.py:85
  108.6 134.5 %all-reduce.8.cloned.1.call-start = ((), (), s32[]{:S(2)}) async-start(), calls=%async_computation.5 | async-start | bytes 4194304 | tf_op jit(solution)/shard_map/psum | solution.py:105
  178.8 147.6 %all-reduce.10.cloned.1.call-start = ((), (), s32[]{:S(2)}) async-start(), calls=%async_computation.6 | async-start | bytes 4194304 | tf_op jit(solution)/shard_map/psum | solution.py:122
  190.1 56.5 %copy-start.58 = (f32[512]{0:T(512)S(1)}, f32[512]{0:T(512)}, u32[]{:S(2)}) copy-start(f32[512]{0:T(512)} %param.23) | copy-start | bytes 6148
  190.1 56.5 %copy-start.63 = (f32[1024]{0:T(1024)S(1)}, f32[1024]{0:T(1024)}, u32[]{:S(2)}) copy-start(f32[1024]{0:T(1024)} %param.25) | copy-start | bytes 12292
  190.1 56.5 %copy-start.64 = (f32[512]{0:T(512)S(1)}, f32[512]{0:T(512)}, u32[]{:S(2)}) copy-start(f32[512]{0:T(512)} %param.24) | copy-start | bytes 6148
  263.3 312.9 %all-reduce.14.cloned.1.call-start = ((), (), s32[]{:S(2)}) async-start(), calls=%async_computation.8 | async-start | bytes 8388608 | tf_op jit(solution)/shard_map/psum | solution.py:112
  343.6 15.5 %copy-start.22 = (f32[32,4,64,64]{3,0,2,1:T(8,128)S(1)}, f32[32,4,64,64]{3,0,2,1:T(8,128)}, u32[]{:S(2)}) copy-start(f32[32,4,64,64]{3,0,2,1:T(8,128)} %copy-done.21) | copy-start | bytes 6291460
  343.6 15.5 %copy-start.23 = (f32[32,64,4,64]{1,0,3,2:T(8,128)S(1)}, f32[32,64,4,64]{1,0,3,2:T(8,128)}, u32[]{:S(2)}) copy-start(f32[32,64,4,64]{1,0,3,2:T(8,128)} %reshape.276) | copy-start | bytes 6291460
  359.1 13.6 %copy-start.35 = (bf16[32,64,4,64]{1,3,2,0:T(8,128)(2,1)S(1)}, bf16[32,64,4,64]{1,3,2,0:T(8,128)(2,1)}, u32[]{:S(2)}) copy-start(bf16[32,64,4,64]{1,3,2,0:T(8,128)(2,1)} %copy.119) | copy-start | bytes 3145732
  467.7 108.4 %copy-start.45 = (f32[2048]{0:T(1024)S(1)}, f32[2048]{0:T(1024)}, u32[]{:S(2)}) copy-start(f32[2048]{0:T(1024)} %copy-done.44) | copy-start | bytes 24580
  467.7 108.4 %copy-start.57 = (f32[512]{0:T(512)S(1)}, f32[512]{0:T(512)}, u32[]{:S(2)}) copy-start(f32[512]{0:T(512)} %param.21) | copy-start | bytes 6148
  467.7 111.9 %copy-start.49 = (f32[2048]{0:T(1024)S(1)}, f32[2048]{0:T(1024)}, u32[]{:S(2)}) copy-start(f32[2048]{0:T(1024)} %copy-done.48) | copy-start | bytes 24580
  467.7 111.9 %copy-start.47 = (f32[2048]{0:T(1024)S(1)}, f32[2048]{0:T(1024)}, u32[]{:S(2)}) copy-start(f32[2048]{0:T(1024)} %copy-done.46) | copy-start | bytes 24580
  600.2 47.1 %all-to-all-start.4 = ((bf16[16,128,512]{2,1,0:T(8,128)(2,1)}), bf16[16,128,512]{2,1,0:T(8,128)(2,1)}, u32[]{:S(2)}, u32[]{:S(2)}) async-start(bf16[16,128,512]{2,1,0:T(8,128)(2,1)} %bitcast.117), calls=%async_computation.4 | async-start | bytes 4194304 | tf_op jit(solution)/shard_map/all_to_all | solution.py:173
  628.0 30.6 %copy-start.27 = (bf16[2048,256]{0,1:T(8,128)(2,1)S(1)}, bf16[2048,256]{0,1:T(8,128)(2,1)}, u32[]{:S(2)}) copy-start(bf16[2048,256]{0,1:T(8,128)(2,1)} %copy-done.26) | copy-start | bytes 3145732
  628.0 33.7 %copy-start.66 = (f32[512]{0:T(512)S(1)}, f32[512]{0:T(512)}, u32[]{:S(2)}) copy-start(f32[512]{0:T(512)} %param.22) | copy-start | bytes 6148
  647.3 264.8 %all-to-all-start.2 = ((bf16[16,128,512]{2,1,0:T(8,128)(2,1)}), bf16[16,128,512]{2,1,0:T(8,128)(2,1)}, u32[]{:S(2)}, u32[]{:S(2)}) async-start(bf16[16,128,512]{2,1,0:T(8,128)(2,1)} %bitcast.115), calls=%async_computation.2 | async-start | bytes 4194304 | tf_op jit(solution)/shard_map/all_to_all | solution.py:172
  658.6 179.0 %all-reduce.12.cloned.1.call-start = ((), (), s32[]{:S(2)}) async-start(), calls=%async_computation.7 | async-start | bytes 12582912 | tf_op jit(solution)/shard_map/psum | solution.py:153
  (55 other events, 277.9 us)
Sparse Core Ops, SparseCore 0:
  178.9 64.1 all-reduce.7
  263.4 62.9 all-reduce.9
  467.9 108.2 all-reduce.13
  667.0 170.4 all-reduce.11
where the time goes:
time: 941 us; the launch traced here: 936 us
  waiting for transfers between devices  427 us (45%)
  local copies, waits for them, and re-layouts  190 us (20%)
  matrix products  148 us (16%)
  blocking collectives  60.4 us (6%)
  other arithmetic  54 us (6%)
  starting transfers between devices  42.2 us (4%)
  between operations  15.1 us (2%)
    psum x1, waiting for transfers between devices, per_device(): lax.psum((grad_qkv, grad_outproj, grad_up, grad_down, grad_up_bias, grad_...  165 us
    psum x1, waiting for transfers between devices, per_device(): lax.psum(ffn_part.astype(jnp.bfloat16), 'tensor').astype(jnp.float32)  108 us
    psum x1, blocking collectives, per_device(): lax.psum((grad_qkv, grad_outproj, grad_up, grad_down, grad_up_bias, grad_...  60.4 us
    psum x1, waiting for transfers between devices, per_device(): lax.psum(second_part.astype(jnp.bfloat16), 'tensor').astype(jnp.float32)  56.8 us
    psum x1, waiting for transfers between devices, per_device(): lax.psum(attn_part.astype(jnp.bfloat16), 'tensor').astype(jnp.float32)  53 us
    dot_general x3, matrix products, linear_attention(): jnp.einsum('chij,cjhf->cihf', scores, values, precision=best)  27.8 us
    dot_general x3, matrix products, linear_attention(): numer = jnp.einsum('cihe,chef->cihf', query, state, precision=best)  27.6 us
    all_to_all x1, waiting for transfers between devices, per_device(): lax.all_to_all(sent[0], 'dp', split_axis=0, concat_axis=0, tiled=True)  24.8 us
  transfers between devices with their start and end apart: 9, of which 6 were waited for; matrix products, arithmetic and copies ran while one was open for 17% of the time, Pallas kernels for 0%

commit v1 on v0

--- a/solution.py
+++ b/solution.py
@@ -5,6 +5,11 @@
 
 HD = 64
 BLK = 64
+
+
+def summed_here(block, axis):
+    blocks = lax.all_gather(block, axis)
+    return jnp.sum(blocks, axis=0)
 
 
 def layer_norm(value, gain, shift):
@@ -119,7 +124,7 @@
     second_part = jnp.einsum(
         "tf,df->td", grad_hidden, up_weight, preferred_element_type=jnp.float32
     )
-    grad_second = lax.psum(second_part.astype(jnp.bfloat16), "tensor").astype(jnp.float32)
+    grad_second = summed_here(second_part.astype(jnp.bfloat16), "tensor").astype(jnp.float32)
     middle_norm, grad_gain_second, grad_shift_second = second_pull(grad_second)
     grad_middle = grad_low.astype(jnp.float32) + middle_norm
     middle_low = grad_middle.astype(jnp.bfloat16)

time: 941 us -> 940 us (level)
    psum x1 -> x0, waiting for transfers between devices: 56.8 us -> none  [per_device(): lax.psum(second_part.astype(jnp.bfloat16), 'tensor').astype(jnp.float32)]
    all_gather x0 -> x1, waiting for transfers between devices: none -> 50.6 us  [summed_here(): blocks = lax.all_gather(block, axis)]
where the time goes in v1:
time: 940 us; the launch traced here: 935 us
  waiting for transfers between devices  420 us (45%)
  local copies, waits for them, and re-layouts  190 us (20%)
  matrix products  148 us (16%)
  blocking collectives  60.4 us (6%)
  other arithmetic  59.1 us (6%)
  starting transfers between devices  42.2 us (4%)
  between operations  15.1 us (2%)
    psum x1, waiting for transfers between devices, per_device(): lax.psum((grad_qkv, grad_outproj, grad_up, grad_down, grad_up_bias, grad_...  165 us
    psum x1, waiting for transfers between devices, per_device(): lax.psum(ffn_part.astype(jnp.bfloat16), 'tensor').astype(jnp.float32)  108 us
    psum x1, blocking collectives, per_device(): lax.psum((grad_qkv, grad_outproj, grad_up, grad_down, grad_up_bias, grad_...  60.4 us
    psum x1, waiting for transfers between devices, per_device(): lax.psum(attn_part.astype(jnp.bfloat16), 'tensor').astype(jnp.float32)  53 us
    all_gather x1, waiting for transfers between devices, summed_here(): blocks = lax.all_gather(block, axis)  50.6 us
    dot_general x3, matrix products, linear_attention(): jnp.einsum('chij,cjhf->cihf', scores, values, precision=best)  27.8 us
    dot_general x3, matrix products, linear_attention(): numer = jnp.einsum('cihe,chef->cihf', query, state, precision=best)  27.6 us
    all_to_all x1, waiting for transfers between devices, per_device(): lax.all_to_all(sent[0], 'dp', split_axis=0, concat_axis=0, tiled=True)  24.8 us
  transfers between devices with their start and end apart: 9, of which 6 were waited for; matrix products, arithmetic and copies ran while one was open for 17% of the time, Pallas kernels for 0%

profile of v1, /device:TPU:0, one launch (start us, length us, event | category | flops | bytes accessed | tf_op | source)
XLA Modules:
  0.0 934.7 jit_solution(4601692308884660456)
XLA Ops:
  13.1 20.6 %gather_fusion.1 = s32[2048]{0:T(1024)} fusion(s32[2048]{0:T(1024)S(1)} %copy-done.2, s32[2048]{0:T(1024)S(1)} %fusion.86), kind=kCustom, calls=%fused_computation.1 | custom fusion | bytes 24576 | tf_op jit(solution)/shard_map/gather | solution.py:86
  33.7 7.4 all-to-all-start.1
  41.0 9.2 gather_fusion
  56.3 11.1 %gather_fusion.5 = bf16[2048,512]{1,0:T(8,128)(2,1)} fusion(bf16[2048,512]{1,0:T(8,128)(2,1)} %param.16, s32[2048]{0:T(1024)S(1)} %fusion.86), kind=kCustom, calls=%fused_computation.5 | custom fusion | bytes 4202496 | tf_op jit(solution)/shard_map/gather | solution.py:85
  72.5 24.8 %all-to-all-done = bf16[16,128,512]{2,1,0:T(8,128)(2,1)S(1)} async-done(((bf16[16,128,512]{2,1,0:T(8,128)(2,1)}), bf16[16,128,512]{2,1,0:T(8,128)(2,1)S(1)}, u32[]{:S(2)}, u32[]{:S(2)}) %all-to-all-start) | async-done | bytes 2097184 | tf_op jit(solution)/shard_map/all_to_all | solution.py:89
  97.4 11.3 %all-to-all-start.3 = ((bf16[16,128,512]{2,1,0:T(8,128)(2,1)}), bf16[16,128,512]{2,1,0:T(8,128)(2,1)}, u32[]{:S(2)}, u32[]{:S(2)}) async-start(bf16[16,128,512]{2,1,0:T(8,128)(2,1)} %bitcast.115), calls=%async_computation.3 | async-start | bytes 4194304 | tf_op jit(solution)/shard_map/all_to_all | solution.py:90
  108.9 9.5 %gather_fusion.2 = bf16[2048,512]{1,0:T(8,128)(2,1)S(1)} fusion(bf16[2048,512]{1,0:T(8,128)(2,1)} %bitcast.114, s32[2048]{0:T(1024)S(1)} %fusion.87), kind=kCustom, calls=%fused_computation.2 | custom fusion | bytes 4202496 | tf_op jit(solution)/shard_map/gather | solution.py:95
  158.4 7.2 fusion.29
  178.8 11.3 %gather_fusion.6 = bf16[2048,512]{1,0:T(8,128)(2,1)} fusion(bf16[2048,512]{1,0:T(8,128)(2,1)} %bitcast.22, s32[2048]{0:T(1024)S(1)} %fusion.87), kind=kCustom, calls=%fused_computation.6 | custom fusion | bytes 4202496 | tf_op jit(solution)/shard_map/gather | solution.py:96
  190.1 53.0 %all-reduce.7.cloned.1.call-done = bf16[2048,512]{1,0:T(8,128)(2,1)} async-done(((bf16[2048,512]{1,0:T(8,128)(2,1)}), bf16[2048,512]{1,0:T(8,128)(2,1)}) %all-reduce.7.cloned.1.call-update) | async-done | bytes 2097168 | tf_op jit(solution)/shard_map/psum | solution.py:110
  269.6 50.6 %all-gather.3.cloned.1.call-done = bf16[4096,512]{1,0:T(8,128)(2,1)} async-done(((bf16[2048,512]{1,0:T(8,128)(2,1)}), bf16[4096,512]{1,0:T(8,128)(2,1)}) %all-gather.3.cloned.1.call-update) | async-done | bytes 4194320 | tf_op jit(solution)/shard_map/all_gather | solution.py:11
  342.4 15.5 %fusion.15 = f32[32,4,64,64]{3,2,1,0:T(8,128)} fusion(f32[32,4,64,64]{2,3,1,0:T(8,128)} %copy-done.30, f32[64,64]{0,1:T(8,128)S(1)} %fusion.79, f32[32,64,4,64]{1,0,3,2:T(8,128)} %reshape.276, f32[32,64,4]{1,2,0:T(4,128)S(1)} %copy-done.53), kind=kOutput, calls=%fused_computation.41 | convolution fusion | flops 403701760 | bytes 6340608 | tf_op jit(solution)/shard_map/transpose(jvp(chij,cjhf->cihf))/dot_general | solution.py:57
  357.9 13.6 %fusion.21 = f32[32,4,64,64]{2,3,1,0:T(8,128)} fusion(f32[32,4,64,64]{3,0,2,1:T(8,128)S(1)} %copy-done.23, f32[32,64,4,64]{1,0,3,2:T(8,128)S(1)} %copy-done.24, f32[32,64,4]{1,2,0:T(4,128)S(1)} %copy-done.53), kind=kOutput, calls=%fused_computation.47 | convolution fusion | flops 403177472 | bytes 6324224 | tf_op jit(solution)/shard_map/transpose(jvp(cihe,chef->cihf))/dot_general | solution.py:56
  378.4 7.5 fusion.19
  436.7 9.9 %add_bitcast_fusion = f32[32,64,4,64]{1,3,2,0:T(8,128)} fusion(f32[32,4,64,64]{2,3,1,0:T(8,128)} %fusion.21, f32[32,4,64,64]{2,3,1,0:T(8,128)} %fusion.19, f32[32,4,64]{2,1,0:T(4,128)S(1)} %copy.105, f32[32,4,64]{2,1,0:T(4,128)S(1)} %get-tuple-element.83, f32[64,64]{0,1:T(8,128)S(1)} %fusion.79, bf16[32,64,4,64]{3,2,1,0:T(4,128)(2,1)} %reshape.267), kind=kOutput, calls=%fused_computation.59 | convolution fusion | flops 405274624 | bytes 7421952 | tf_op jit(solution)/shard_map/transpose(jvp(cihe,cjhe->chij))/dot_general | solution.py:53
  467.3 107.7 %all-reduce.11.cloned.1.call-done = (bf16[2048,512]{1,0:T(8,128)(2,1)}, bf16[2048,512]{1,0:T(8,128)(2,1)}) async-done(((bf16[2048,512]{1,0:T(8,128)(2,1)}, bf16[2048,512]{1,0:T(8,128)(2,1)}), (bf16[2048,512]{1,0:T(8,128)(2,1)}, bf16[2048,512]{1,0:T(8,128)(2,1)})) %all-reduce.11.cloned.1.call-update) | async-done | bytes 4194320 | tf_op jit(solution)/shard_map/psum | solution.py:117
  587.9 11.1 %gather_fusion.7 = bf16[2048,512]{1,0:T(8,128)(2,1)} fusion(bf16[2048,512]{1,0:T(8,128)(2,1)} %get-tuple-element.80, s32[2048]{0:T(1024)S(1)} %broadcast_clamp_fusion), kind=kCustom, calls=%fused_computation.7 | custom fusion | bytes 4202496 | tf_op jit(solution)/shard_map/gather | solution.py:174
  615.7 11.1 %gather_fusion.3 = bf16[2048,512]{1,0:T(8,128)(2,1)} fusion(bf16[2048,512]{1,0:T(8,128)(2,1)} %get-tuple-element.81, s32[2048]{0:T(1024)S(1)} %broadcast_clamp_fusion), kind=kCustom, calls=%fused_computation.3 | custom fusion | bytes 4202496 | tf_op jit(solution)/shard_map/gather | solution.py:173
  626.9 19.3 %all-to-all-done.4 = bf16[16,128,512]{2,1,0:T(8,128)(2,1)} async-done(((bf16[16,128,512]{2,1,0:T(8,128)(2,1)}), bf16[16,128,512]{2,1,0:T(8,128)(2,1)}, u32[]{:S(2)}, u32[]{:S(2)}) %all-to-all-start.4) | async-done | bytes 2097184 | tf_op jit(solution)/shard_map/all_to_all | solution.py:178
  646.1 11.3 %all-to-all-start.2 = ((bf16[16,128,512]{2,1,0:T(8,128)(2,1)}), bf16[16,128,512]{2,1,0:T(8,128)(2,1)}, u32[]{:S(2)}, u32[]{:S(2)}) async-start(bf16[16,128,512]{2,1,0:T(8,128)(2,1)} %bitcast.116), calls=%async_computation.2 | async-start | bytes 4194304 | tf_op jit(solution)/shard_map/all_to_all | solution.py:177
  671.4 164.9 %all-reduce.9.cloned.1.call-done = (f32[3,512,256]{1,2,0:T(8,128)}, f32[256,512]{1,0:T(8,128)}, f32[512,1024]{1,0:T(8,128)}, f32[1024,512]{1,0:T(8,128)}) async-done(((f32[3,512,256]{1,2,0:T(8,128)}, f32[256,512]{1,0:T(8,128)}, f32[512,1024]{1,0:T(8,128)}, f32[1024,512]{1,0:T(8,128)}), (f32[3,512,256]{1,2,0:T(8,128)}, f32[256,512]{1,0:T(8,128)}, f32[512,1024]{1,0:T(8,128)}, ...) | async-done | bytes 6291472 | tf_op jit(solution)/shard_map/psum | solution.py:158
  839.4 60.4 %all-reduce = (f32[512]{0:T(512)}, f32[512]{0:T(512)}, f32[512]{0:T(512)}, f32[512]{0:T(512)}, f32[1024]{0:T(1024)}) all-reduce(f32[512]{0:T(512)S(1)} %get-tuple-element.52, f32[512]{0:T(512)S(1)} %get-tuple-element.55, f32[512]{0:T(512)S(1)} %get-tuple-element.50, ...), channel_id=1, replica_groups=mesh['dp'=16,'tensor'=2] {'dp'}, use_global_device_ids=true, to_apply=%region_23.24 | all-reduce | flops 3072 | bytes 24576 | tf_op jit(solution)/shard_map/psum | solution.py:158
  899.8 11.1 %gather_fusion.8 = bf16[2048,512]{1,0:T(8,128)(2,1)} fusion(bf16[2048,512]{1,0:T(8,128)(2,1)} %bitcast.38, s32[2048]{0:T(1024)S(1)} %fusion.88), kind=kCustom, calls=%fused_computation.8 | custom fusion | bytes 4202496 | tf_op jit(solution)/shard_map/gather | solution.py:182
  910.9 11.2 %gather_fusion.4 = bf16[2048,512]{1,0:T(8,128)(2,1)} fusion(bf16[2048,512]{1,0:T(8,128)(2,1)} %bitcast.20, s32[2048]{0:T(1024)S(1)} %fusion.88), kind=kCustom, calls=%fused_computation.4 | custom fusion | bytes 4202496 | tf_op jit(solution)/shard_map/gather | solution.py:181
  (238 shorter events, 249.3 us)
Async XLA Ops:
  7.2 33.9 %copy-start = (bf16[2048,512]{1,0:T(8,128)(2,1)S(1)}, bf16[2048,512]{1,0:T(8,128)(2,1)}, u32[]{:S(2)}) copy-start(bf16[2048,512]{1,0:T(8,128)(2,1)} %param.13) | copy-start | bytes 6291460
  13.1 20.6 %copy-start.54 = (s32[2048]{0:T(1024)}, s32[2048]{0:T(1024)S(1)}, u32[]{:S(2)}) copy-start(s32[2048]{0:T(1024)S(1)} %get-tuple-element.14) | copy-start | bytes 24580
  33.7 16.6 %all-to-all-start.1 = ((s32[16,1,128]{2,1,0:T(1,128)}), s32[16,1,128]{2,1,0:T(1,128)S(1)}, u32[]{:S(2)}, u32[]{:S(2)}) async-start(s32[16,1,128]{2,1,0:T(1,128)} %bitcast.2), calls=%async_computation.1 | async-start | bytes 16384 | tf_op jit(solution)/shard_map/all_to_all | solution.py:91
  50.2 17.2 %copy-start.50 = (s32[16,1,128]{2,1,0:T(1,128)}, s32[16,1,128]{2,1,0:T(1,128)S(1)}, u32[]{:S(2)}) copy-start(s32[16,1,128]{2,1,0:T(1,128)S(1)} %all-to-all-done.1) | copy-start | bytes 24580
  50.2 47.1 %all-to-all-start = ((bf16[16,128,512]{2,1,0:T(8,128)(2,1)}), bf16[16,128,512]{2,1,0:T(8,128)(2,1)S(1)}, u32[]{:S(2)}, u32[]{:S(2)}) async-start(bf16[16,128,512]{2,1,0:T(8,128)(2,1)} %bitcast.117), calls=%async_computation | async-start | bytes 4194304 | tf_op jit(solution)/shard_map/all_to_all | solution.py:89
  97.4 81.4 %all-to-all-start.3 = ((bf16[16,128,512]{2,1,0:T(8,128)(2,1)}), bf16[16,128,512]{2,1,0:T(8,128)(2,1)}, u32[]{:S(2)}, u32[]{:S(2)}) async-start(bf16[16,128,512]{2,1,0:T(8,128)(2,1)} %bitcast.115), calls=%async_computation.3 | async-start | bytes 4194304 | tf_op jit(solution)/shard_map/all_to_all | solution.py:90
  108.6 134.5 %all-reduce.7.cloned.1.call-start = ((), (), s32[]{:S(2)}) async-start(), calls=%async_computation.5 | async-start | bytes 4194304 | tf_op jit(solution)/shard_map/psum | solution.py:110
  178.8 141.4 %all-gather.3.cloned.1.call-start = ((), (), s32[]{:S(2)}) async-start(), calls=%async_computation.6 | async-start | bytes 6291456 | tf_op jit(solution)/shard_map/all_gather | solution.py:11
  190.1 56.5 %copy-start.58 = (f32[512]{0:T(512)S(1)}, f32[512]{0:T(512)}, u32[]{:S(2)}) copy-start(f32[512]{0:T(512)} %param.23) | copy-start | bytes 6148
  190.1 56.5 %copy-start.63 = (f32[1024]{0:T(1024)S(1)}, f32[1024]{0:T(1024)}, u32[]{:S(2)}) copy-start(f32[1024]{0:T(1024)} %param.25) | copy-start | bytes 12292
  190.1 56.5 %copy-start.64 = (f32[512]{0:T(512)S(1)}, f32[512]{0:T(512)}, u32[]{:S(2)}) copy-start(f32[512]{0:T(512)} %param.24) | copy-start | bytes 6148
  263.3 311.7 %all-reduce.11.cloned.1.call-start = ((), (), s32[]{:S(2)}) async-start(), calls=%async_computation.8 | async-start | bytes 8388608 | tf_op jit(solution)/shard_map/psum | solution.py:117
  342.4 15.5 %copy-start.23 = (f32[32,4,64,64]{3,0,2,1:T(8,128)S(1)}, f32[32,4,64,64]{3,0,2,1:T(8,128)}, u32[]{:S(2)}) copy-start(f32[32,4,64,64]{3,0,2,1:T(8,128)} %copy-done.22) | copy-start | bytes 6291460
  342.4 15.5 %copy-start.24 = (f32[32,64,4,64]{1,0,3,2:T(8,128)S(1)}, f32[32,64,4,64]{1,0,3,2:T(8,128)}, u32[]{:S(2)}) copy-start(f32[32,64,4,64]{1,0,3,2:T(8,128)} %reshape.276) | copy-start | bytes 6291460
  357.9 13.6 %copy-start.35 = (bf16[32,64,4,64]{1,3,2,0:T(8,128)(2,1)S(1)}, bf16[32,64,4,64]{1,3,2,0:T(8,128)(2,1)}, u32[]{:S(2)}) copy-start(bf16[32,64,4,64]{1,3,2,0:T(8,128)(2,1)} %copy.119) | copy-start | bytes 3145732
  466.6 108.4 %copy-start.45 = (f32[2048]{0:T(1024)S(1)}, f32[2048]{0:T(1024)}, u32[]{:S(2)}) copy-start(f32[2048]{0:T(1024)} %copy-done.44) | copy-start | bytes 24580
  466.6 108.4 %copy-start.57 = (f32[512]{0:T(512)S(1)}, f32[512]{0:T(512)}, u32[]{:S(2)}) copy-start(f32[512]{0:T(512)} %param.21) | copy-start | bytes 6148
  466.6 111.9 %copy-start.49 = (f32[2048]{0:T(1024)S(1)}, f32[2048]{0:T(1024)}, u32[]{:S(2)}) copy-start(f32[2048]{0:T(1024)} %copy-done.48) | copy-start | bytes 24580
  466.6 111.9 %copy-start.47 = (f32[2048]{0:T(1024)S(1)}, f32[2048]{0:T(1024)}, u32[]{:S(2)}) copy-start(f32[2048]{0:T(1024)} %copy-done.46) | copy-start | bytes 24580
  599.1 47.1 %all-to-all-start.4 = ((bf16[16,128,512]{2,1,0:T(8,128)(2,1)}), bf16[16,128,512]{2,1,0:T(8,128)(2,1)}, u32[]{:S(2)}, u32[]{:S(2)}) async-start(bf16[16,128,512]{2,1,0:T(8,128)(2,1)} %bitcast.118), calls=%async_computation.4 | async-start | bytes 4194304 | tf_op jit(solution)/shard_map/all_to_all | solution.py:178
  626.9 30.6 %copy-start.28 = (bf16[2048,256]{0,1:T(8,128)(2,1)S(1)}, bf16[2048,256]{0,1:T(8,128)(2,1)}, u32[]{:S(2)}) copy-start(bf16[2048,256]{0,1:T(8,128)(2,1)} %copy-done.27) | copy-start | bytes 3145732
  626.9 33.7 %copy-start.66 = (f32[512]{0:T(512)S(1)}, f32[512]{0:T(512)}, u32[]{:S(2)}) copy-start(f32[512]{0:T(512)} %param.22) | copy-start | bytes 6148
  646.1 264.8 %all-to-all-start.2 = ((bf16[16,128,512]{2,1,0:T(8,128)(2,1)}), bf16[16,128,512]{2,1,0:T(8,128)(2,1)}, u32[]{:S(2)}, u32[]{:S(2)}) async-start(bf16[16,128,512]{2,1,0:T(8,128)(2,1)} %bitcast.116), calls=%async_computation.2 | async-start | bytes 4194304 | tf_op jit(solution)/shard_map/all_to_all | solution.py:177
  657.4 178.9 %all-reduce.9.cloned.1.call-start = ((), (), s32[]{:S(2)}) async-start(), calls=%async_computation.7 | async-start | bytes 12582912 | tf_op jit(solution)/shard_map/psum | solution.py:158
  (55 other events, 278.1 us)
Sparse Core Ops, SparseCore 0:
  178.9 64.1 all-reduce.6
  263.4 56.7 all-gather.2
  466.7 108.2 all-reduce.10
  665.9 170.4 all-reduce.8
